TPU v7x, 32 devices: a whole 2x2x4 slice. The times are simulated.
32 devices in a mesh: fsdp: 4 (over y, x), ctx: 2 (over core), tp: 4 (over z).
Axes of the slice: x: 2, y: 2, z: 4, core: 2. Of those that a mesh axis runs over, the one named last changes fastest.
Arguments:
- residual: bfloat16 [8192, 2048], P(('fsdp', 'ctx'), 'tp'), may hold values from -6 to 6
- out_grad: bfloat16 [8192, 2048], P(('fsdp', 'ctx'), 'tp'), may hold values from -6 to 6
- path_depth: int32 [8192], P(('fsdp', 'ctx')), may hold values from 0 to 895, as said below
- seg_lengths: int32 [4, 13], P('fsdp'), may hold values from 64 to 512, as said below
- parents: int32 [4, 13], P('fsdp'), may hold values from 0 to 4, as said below
- attn_norm_gain: bfloat16 [2048], P('tp'), may hold values from 0.099609375 to 1.8984375
- attn_norm_bias: bfloat16 [2048], P('tp'), may hold values from -1.5 to 1.5
- ffn_norm_gain: bfloat16 [2048], P('tp'), may hold values from 0.099609375 to 1.8984375
- ffn_norm_bias: bfloat16 [2048], P('tp'), may hold values from -1.5 to 1.5
- qkv_weight: bfloat16 [2048, 6144], P(('fsdp', 'ctx'), 'tp'), may hold values from -0.125 to 0.125
- qkv_bias: bfloat16 [6144], P('tp'), may hold values from -2.5 to 2.5
- dense_weight: bfloat16 [2048, 2048], P('tp', ('fsdp', 'ctx')), may hold values from -2 to 2
- dense_bias: bfloat16 [2048], P('tp'), may hold values from -2.5 to 2.5
- up_weight: bfloat16 [2048, 8192], P(('fsdp', 'ctx'), 'tp'), may hold values from -0.125 to 0.125
- up_bias: bfloat16 [8192], P('tp'), may hold values from -2.5 to 2.5
- down_weight: bfloat16 [8192, 2048], P('tp', ('fsdp', 'ctx')), may hold values from -0.0625 to 0.0625
- down_bias: bfloat16 [2048], P('tp'), may hold values from -2.5 to 2.5
Outputs:
- output: bfloat16 [8192, 2048], P(('fsdp', 'ctx'), 'tp')
- input_grad: bfloat16 [8192, 2048], P(('fsdp', 'ctx'), 'tp')
- grad_attn_norm_gain: float32 [2048], P('tp')
- grad_attn_norm_bias: float32 [2048], P('tp')
- grad_ffn_norm_gain: float32 [2048], P('tp')
- grad_ffn_norm_bias: float32 [2048], P('tp')
- grad_qkv_weight: float32 [2048, 6144], P(('fsdp', 'ctx'), 'tp')
- grad_qkv_bias: float32 [6144], P('tp')
- grad_dense_weight: float32 [2048, 2048], P('tp', ('fsdp', 'ctx'))
- grad_dense_bias: float32 [2048], P('tp')
- grad_up_weight: float32 [2048, 8192], P(('fsdp', 'ctx'), 'tp')
- grad_up_bias: float32 [8192], P('tp')
- grad_down_weight: float32 [8192, 2048], P('tp', ('fsdp', 'ctx'))
- grad_down_bias: float32 [2048], P('tp')
Inputs may be any that keep to these rules, and one draw needn't show every extreme that they name: `seg_lengths`: row t lists tree t's segments in order: the trunk of 512 tokens, 4 branches, then 8 leaves; each row sums to 2048. `parents`: entry s of row t is the segment that segment s hangs from: 0 for the trunk itself and for each branch, a branch for each leaf; each branch holds exactly two leaves. `path_depth`: A token's place within its segment plus the lengths of the segment's proper ancestors in its tree.
All inputs are finite; a program needn't handle non-finite values.
Results may differ from a plain program's by a relative error of at most 0.012.
Values may be sent and summed in bfloat16 or wider, within the bound.
No kernel may reach another device: no remote copies, remote signals or barrier semaphores. Data moves between devices by JAX's collectives and lax.ppermute only.
A program may use at most 256 MiB of HBM per device.

v0:
```python
from functools import partial
import math
import jax
import jax.numpy as jnp
from jax import lax
from jax.sharding import PartitionSpec as P

HEAD_DIM = 256
ROTARY = 64
SEGS = 13
norm_epsilon = 1e-05
masked_score = -1e30
block_limit = 512


def from_behind(x, axis, by):
    peers = lax.axis_size(axis)
    pairs = [(i, i + by) for i in range(peers) if 0 <= i + by < peers]
    return lax.ppermute(x, axis, pairs)


def rotary(vectors, places):
    half_rot = ROTARY // 2
    frequency = jnp.power(10000.0, -2.0 * jnp.arange(half_rot).astype(jnp.float32) / ROTARY)
    angles = places.astype(jnp.float32)[:, None] * frequency[None, :]
    cosine = jnp.cos(angles)[:, None, :]
    sine_part = jnp.sin(angles)[:, None, :]
    first_half = vectors[..., :half_rot]
    second_half = vectors[..., half_rot:ROTARY]
    return jnp.concatenate(
        [
            first_half * cosine - second_half * sine_part,
            second_half * cosine + first_half * sine_part,
            vectors[..., ROTARY:],
        ],
        axis=-1,
    )


def tree_tables(lengths, parent):
    starts = jnp.cumsum(lengths) - lengths
    labels = jnp.arange(SEGS)
    grand_parent = jnp.sum(
        jnp.where(parent[:, None] == labels[None, :], parent[None, :], 0), axis=1
    )
    ancestor = (
        (labels[None, :] == labels[:, None])
        | (labels[None, :] == parent[:, None])
        | (labels[None, :] == grand_parent[:, None])
    )
    return (starts, ancestor.astype(jnp.float32))


def segment_onehot(places, starts):
    membership = jnp.sum((places[:, None] >= starts[None, :]).astype(jnp.int32), axis=1) - 1
    return (membership[:, None] == jnp.arange(SEGS)[None, :]).astype(jnp.float32)


def visible(hot_query, place_query, hot_key, place_key, ancestor):
    reachable = jnp.dot(jnp.dot(hot_query, ancestor), hot_key.T)
    return (reachable > 0.5) & (place_key[None, :] <= place_query[:, None])


def on_device(
    residual,
    out_grad,
    path_depth,
    seg_lengths,
    parents,
    attn_norm_gain,
    attn_norm_bias,
    ffn_norm_gain,
    ffn_norm_bias,
    qkv_weight,
    qkv_bias,
    dense_weight,
    dense_bias,
    up_weight,
    up_bias,
    down_weight,
    down_bias,
):
    row_count = residual.shape[0]
    local_width = residual.shape[1]
    head_count = qkv_weight.shape[1] // (3 * HEAD_DIM)
    score_scale = 1.0 / math.sqrt(HEAD_DIM)
    ctx_index = lax.axis_index("ctx")
    tp_index = lax.axis_index("tp")
    norm_stack = jnp.stack([attn_norm_gain, attn_norm_bias, ffn_norm_gain, ffn_norm_bias])
    full_rows, norm_terms = (
        lax.all_gather(residual, "tp", axis=1, tiled=True),
        lax.all_gather(norm_stack, "tp", axis=1, tiled=True),
    )
    norm_terms = norm_terms.astype(jnp.float32)
    qkv_full, up_full = (
        lax.all_gather(qkv_weight, ("fsdp", "ctx"), axis=0, tiled=True),
        lax.all_gather(up_weight, ("fsdp", "ctx"), axis=0, tiled=True),
    )
    dense_full, down_full = (
        lax.all_gather(dense_weight, ("fsdp", "ctx"), axis=1, tiled=True),
        lax.all_gather(down_weight, ("fsdp", "ctx"), axis=1, tiled=True),
    )
    rows_wide = full_rows.astype(jnp.float32)
    centred = rows_wide - jnp.mean(rows_wide, axis=1, keepdims=True)
    inverse_scale = lax.rsqrt(jnp.mean(centred * centred, axis=1, keepdims=True) + norm_epsilon)
    normed = centred * inverse_scale
    attn_in = (normed * norm_terms[0] + norm_terms[1]).astype(jnp.bfloat16)
    ffn_in = (normed * norm_terms[2] + norm_terms[3]).astype(jnp.bfloat16)
    joined = (
        jnp.dot(attn_in, qkv_full, preferred_element_type=jnp.float32)
        + qkv_bias.astype(jnp.float32)
    ).reshape(row_count, head_count, 3, HEAD_DIM)
    queries_pre = joined[:, :, 0]
    query_rows = rotary(queries_pre, path_depth).astype(jnp.bfloat16)
    key_rows = rotary(joined[:, :, 1], path_depth).astype(jnp.bfloat16)
    value_rows = joined[:, :, 2].astype(jnp.bfloat16)
    far_keys, far_values = from_behind((key_rows, value_rows), "ctx", 1)
    starts, ancestor = tree_tables(seg_lengths[0], parents[0])
    places = ctx_index * row_count + jnp.arange(row_count, dtype=jnp.int32)
    key_places = jnp.concatenate([places - row_count, places])
    hot_query = segment_onehot(places, starts)
    hot_key = segment_onehot(key_places, starts)
    all_keys = jnp.concatenate([far_keys, key_rows], axis=0)
    all_values = jnp.concatenate([far_values, value_rows], axis=0)
    block_starts = list(range(0, row_count, block_limit))

    def block_scores(block_start, block_size, key_set):
        key_span = row_count + block_start + block_size
        query_block = query_rows[block_start : block_start + block_size]
        scores = (
            jnp.einsum(
                "nhe,lhe->hnl", query_block, key_set[:key_span], preferred_element_type=jnp.float32
            )
            * score_scale
        )
        reachable = visible(
            hot_query[block_start : block_start + block_size],
            places[block_start : block_start + block_size],
            hot_key[:key_span],
            key_places[:key_span],
            ancestor,
        )
        return jnp.where(reachable[None], scores, masked_score)

    out_blocks = []
    log_totals = []
    for block_start in block_starts:
        block_size = min(block_limit, row_count - block_start)
        key_span = row_count + block_start + block_size
        scores = block_scores(block_start, block_size, all_keys)
        row_top = jnp.max(scores, axis=-1, keepdims=True)
        exp_scores = jnp.exp(scores - row_top)
        exp_total = jnp.sum(exp_scores, axis=-1, keepdims=True)
        attn_probs = exp_scores / exp_total
        out_blocks.append(
            jnp.einsum(
                "hnl,lhe->nhe",
                attn_probs.astype(jnp.bfloat16),
                all_values[:key_span],
                preferred_element_type=jnp.float32,
            )
        )
        log_totals.append(row_top + jnp.log(exp_total))
    attended = (
        jnp.concatenate(out_blocks, axis=0)
        .reshape(row_count, head_count * HEAD_DIM)
        .astype(jnp.bfloat16)
    )
    hidden_pre = jnp.dot(ffn_in, up_full, preferred_element_type=jnp.float32) + up_bias.astype(
        jnp.float32
    )
    hidden_wide, gelu_back = jax.vjp(partial(jax.nn.gelu, approximate=False), hidden_pre)
    hidden = hidden_wide.astype(jnp.bfloat16)
    partial_out = jnp.dot(attended, dense_full, preferred_element_type=jnp.float32) + jnp.dot(
        hidden, down_full, preferred_element_type=jnp.float32
    )
    shared_out = lax.psum_scatter(partial_out, "tp", scatter_dimension=1, tiled=True)
    output = (
        residual.astype(jnp.float32)
        + shared_out
        + dense_bias.astype(jnp.float32)
        + down_bias.astype(jnp.float32)
    ).astype(jnp.bfloat16)
    cotangent = lax.all_gather(out_grad, "tp", axis=1, tiled=True)
    grad_out_bias = jnp.sum(out_grad.astype(jnp.float32), axis=0)
    grad_dense_w = jnp.einsum("rf,rd->fd", attended, cotangent, preferred_element_type=jnp.float32)
    grad_down_w = jnp.einsum("rf,rd->fd", hidden, cotangent, preferred_element_type=jnp.float32)
    grad_attended = jnp.einsum(
        "rd,fd->rf", cotangent, dense_full, preferred_element_type=jnp.float32
    ).astype(jnp.bfloat16)
    grad_hidden = jnp.einsum("rd,fd->rf", cotangent, down_full, preferred_element_type=jnp.float32)
    grad_pre = gelu_back(grad_hidden)[0].astype(jnp.bfloat16)
    grad_up_w = jnp.einsum("rd,rf->df", ffn_in, grad_pre, preferred_element_type=jnp.float32)
    grad_up_b = jnp.sum(grad_pre.astype(jnp.float32), axis=0)
    grad_ffn_in = jnp.einsum("rf,df->rd", grad_pre, up_full, preferred_element_type=jnp.float32)
    key_set = all_keys
    grad_att_heads = grad_attended.reshape(row_count, head_count, HEAD_DIM)
    grad_query_parts = []
    grad_key_all = jnp.zeros((2 * row_count, head_count, HEAD_DIM), jnp.float32)
    grad_value_all = jnp.zeros((2 * row_count, head_count, HEAD_DIM), jnp.float32)
    for block_number, block_start in enumerate(block_starts):
        block_size = min(block_limit, row_count - block_start)
        key_span = row_count + block_start + block_size
        scores = block_scores(block_start, block_size, key_set)
        attn_probs = jnp.exp(scores - log_totals[block_number])
        grad_block = grad_att_heads[block_start : block_start + block_size]
        grad_value_all = grad_value_all.at[:key_span].add(
            jnp.einsum(
                "hnl,nhe->lhe",
                attn_probs.astype(jnp.bfloat16),
                grad_block,
                preferred_element_type=jnp.float32,
            )
        )
        grad_dots = jnp.einsum(
            "nhe,lhe->hnl", grad_block, all_values[:key_span], preferred_element_type=jnp.float32
        )
        row_delta = jnp.sum(attn_probs * grad_dots, axis=-1, keepdims=True)
        grad_scores = (attn_probs * (grad_dots - row_delta)).astype(jnp.bfloat16)
        grad_query_parts.append(
            jnp.einsum(
                "hnl,lhe->nhe", grad_scores, key_set[:key_span], preferred_element_type=jnp.float32
            )
            * score_scale
        )
        grad_key_all = grad_key_all.at[:key_span].add(
            jnp.einsum(
                "hnl,nhe->lhe",
                grad_scores,
                query_rows[block_start : block_start + block_size],
                preferred_element_type=jnp.float32,
            )
            * score_scale
        )
    arriving_keys, arriving_values = from_behind(
        (grad_key_all[:row_count], grad_value_all[:row_count]), "ctx", -1
    )
    grad_keys = grad_key_all[row_count:] + arriving_keys
    grad_values = grad_value_all[row_count:] + arriving_values
    grad_queries = jnp.concatenate(grad_query_parts, axis=0)
    rotated_unused, rotary_back = jax.vjp(lambda vectors: rotary(vectors, path_depth), queries_pre)
    grad_joined = (
        jnp.stack([rotary_back(grad_queries)[0], rotary_back(grad_keys)[0], grad_values], axis=2)
        .astype(jnp.bfloat16)
        .reshape(row_count, head_count * 3 * HEAD_DIM)
    )
    grad_qkv_w = jnp.einsum("rd,rf->df", attn_in, grad_joined, preferred_element_type=jnp.float32)
    grad_qkv_b = jnp.sum(grad_joined.astype(jnp.float32), axis=0)
    grad_attn_in = jnp.einsum(
        "rf,df->rd", grad_joined, qkv_full, preferred_element_type=jnp.float32
    )
    total_attn, total_ffn = lax.psum((grad_attn_in, grad_ffn_in), "tp")

    def norm_back(total_grad, gain_row):
        scaled = total_grad * gain_row
        mean_plain = jnp.mean(scaled, axis=1, keepdims=True)
        mean_normed = jnp.mean(scaled * normed, axis=1, keepdims=True)
        back_rows = inverse_scale * (scaled - mean_plain - normed * mean_normed)
        gain_grad = jnp.sum(total_grad * normed, axis=0)
        shift_grad = jnp.sum(total_grad, axis=0)
        return (
            lax.dynamic_slice_in_dim(back_rows, tp_index * local_width, local_width, 1),
            lax.dynamic_slice_in_dim(gain_grad, tp_index * local_width, local_width, 0),
            lax.dynamic_slice_in_dim(shift_grad, tp_index * local_width, local_width, 0),
        )

    back_attn, attn_gain_grad, attn_shift_grad = norm_back(total_attn, norm_terms[0])
    back_ffn, ffn_gain_grad, ffn_shift_grad = norm_back(total_ffn, norm_terms[2])
    norm_grads = jnp.stack([attn_gain_grad, attn_shift_grad, ffn_gain_grad, ffn_shift_grad])
    back_total = back_attn + back_ffn
    input_grad = (out_grad.astype(jnp.float32) + back_total).astype(jnp.bfloat16)
    qkv_bias_grad, up_bias_grad, out_bias_grad, norm_totals = lax.psum(
        (grad_qkv_b, grad_up_b, grad_out_bias, norm_grads), ("fsdp", "ctx")
    )
    qkv_weight_grad, up_weight_grad = (
        lax.psum_scatter(
            grad_qkv_w.astype(jnp.bfloat16), ("fsdp", "ctx"), scatter_dimension=0, tiled=True
        ).astype(jnp.float32),
        lax.psum_scatter(
            grad_up_w.astype(jnp.bfloat16), ("fsdp", "ctx"), scatter_dimension=0, tiled=True
        ).astype(jnp.float32),
    )
    dense_weight_grad, down_weight_grad = (
        lax.psum_scatter(
            grad_dense_w.astype(jnp.bfloat16), ("fsdp", "ctx"), scatter_dimension=1, tiled=True
        ).astype(jnp.float32),
        lax.psum_scatter(
            grad_down_w.astype(jnp.bfloat16), ("fsdp", "ctx"), scatter_dimension=1, tiled=True
        ).astype(jnp.float32),
    )
    return (
        output,
        input_grad,
        norm_totals[0],
        norm_totals[1],
        norm_totals[2],
        norm_totals[3],
        qkv_weight_grad,
        qkv_bias_grad,
        dense_weight_grad,
        out_bias_grad,
        up_weight_grad,
        up_bias_grad,
        down_weight_grad,
        out_bias_grad,
    )


def solution(mesh):
    placed = (
        P(("fsdp", "ctx"), "tp"),
        P(("fsdp", "ctx"), "tp"),
        P(("fsdp", "ctx")),
        P("fsdp", None),
        P("fsdp", None),
        P("tp"),
        P("tp"),
        P("tp"),
        P("tp"),
        P(("fsdp", "ctx"), "tp"),
        P("tp"),
        P("tp", ("fsdp", "ctx")),
        P("tp"),
        P(("fsdp", "ctx"), "tp"),
        P("tp"),
        P("tp", ("fsdp", "ctx")),
        P("tp"),
    )
    return jax.shard_map(
        on_device,
        mesh=mesh,
        in_specs=placed,
        out_specs=(
            P(("fsdp", "ctx"), "tp"),
            P(("fsdp", "ctx"), "tp"),
            P("tp"),
            P("tp"),
            P("tp"),
            P("tp"),
            P(("fsdp", "ctx"), "tp"),
            P("tp"),
            P("tp", ("fsdp", "ctx")),
            P("tp"),
            P(("fsdp", "ctx"), "tp"),
            P("tp"),
            P("tp", ("fsdp", "ctx")),
            P("tp"),
        ),
        check_vma=False,
    )
```

profile of v0, /device:TPU:0, one launch (start us, length us, event | category | flops | bytes accessed | tf_op | source)
XLA Modules:
  0.0 1348.0 jit_solution(2497140615921052916)
XLA Ops:
  19.3 15.1 %all_gather.22 = bf16[4,2048]{1,0:T(4,128)(2,1)S(1)} all-gather(bf16[4,512]{1,0:T(4,128)(2,1)S(1)} %pad_maximum_fusion.16), channel_id=1, replica_groups=mesh['fsdp'=4,'ctx'=2,'tp'=4] {'tp'}, dimensions={1}, use_global_device_ids=true | all-gather | bytes 20480 | tf_op jit(solution)/shard_map/all_gather | solution.py:92
  42.4 50.9 %all-gather.7.cloned.1.call-done = bf16[1024,2048]{1,0:T(8,128)(2,1)} async-done(((bf16[1024,512]{1,0:T(8,128)(2,1)}), bf16[1024,2048]{1,0:T(8,128)(2,1)}) %all-gather.7.cloned.1.call-update) | async-done | bytes 4194320 | tf_op jit(solution)/shard_map/all_gather | solution.py:91
  98.0 41.3 %all-gather.9.cloned.1.call-done = bf16[2048,1536]{1,0:T(8,128)(2,1)} async-done(((bf16[256,1536]{1,0:T(8,128)(2,1)}), bf16[2048,1536]{1,0:T(8,128)(2,1)}) %all-gather.9.cloned.1.call-update) | async-done | bytes 6291472 | tf_op jit(solution)/shard_map/all_gather | solution.py:96
  139.3 12.4 convolution_add_fusion
  151.7 6.6 copy.87
  177.5 74.1 %all-gather.17.cloned.1.call-done = bf16[1024,2048]{1,0:T(8,128)(2,1)} async-done(((bf16[1024,512]{1,0:T(8,128)(2,1)}), bf16[1024,2048]{1,0:T(8,128)(2,1)}) %all-gather.17.cloned.1.call-update) | async-done | bytes 4194320 | tf_op jit(solution)/shard_map/all_gather | solution.py:184
  251.6 5.2 convolution_convert_fusion.4
  292.9 5.3 bitcast_add_fusion.1
  331.8 13.6 %convolution_convert_fusion.2 = bf16[2048,1536]{1,0:T(8,128)(2,1)} fusion(bf16[1024,1536]{0,1:T(8,128)(2,1)} %bitcast.86, bf16[1024,2048]{1,0:T(8,128)(2,1)} %all-gather.7.cloned.1.call-done, f32[2048]{0:T(1024)S(1)} %bitcast.101, f32[2048]{0:T(1024)S(1)} %bitcast.89, f32[1024]{0:T(1024)S(1)} %add_rsqrt_fusion, f32[1024]{0:T(1024)S(1)} %broadcast_multiply_fusion.6), kind=kOutput, calls=%fused_computation.37 | convolution fusion | flops 6458179584 | bytes 13656064 | tf_op jit(solution)/shard_map/rd,rf->df/dot_general | solution.py:247
  346.1 14.9 %fusion.65 = f32[1024,2048]{1,0:T(8,128)} fusion(bf16[2048,2048]{1,0:T(8,128)(2,1)} %all-gather.13.cloned.1.call-done, bf16[1024,2048]{1,0:T(8,128)(2,1)} %all-gather.7.cloned.1.call-done, f32[2048]{0:T(1024)S(1)} %bitcast.98, f32[2048]{0:T(1024)S(1)} %bitcast.91, f32[1024]{0:T(1024)S(1)} %add_rsqrt_fusion, f32[1024]{0:T(1024)S(1)} %broadcast_multiply_fusion.6), kind=kOutput, calls=%fused_computation.166 | convolution fusion | flops 8602517504 | bytes 20996096 | tf_op jit(solution)/shard_map/dot_general | solution.py:169
  366.0 33.7 %convert_reduce_fusion.1 = (f32[2048]{0:T(1024)S(1)}, bf16[1024,2048]{1,0:T(8,128)(2,1)}, f32[1024,2048]{1,0:T(8,128)}) fusion(f32[1024,2048]{1,0:T(8,128)} %fusion.65, f32[2048]{0:T(1024)S(1)} %copy-done.36, bf16[1024,2048]{1,0:T(8,128)(2,1)} %all-gather.17.cloned.1.call-done, bf16[2048,2048]{1,0:T(8,128)(2,1)} %all-gather.15.cloned.1.call-done), kind=kOutput, calls=%fused_computation.7 | convolution fusion | flops 8747218944 | bytes 33570816 | tf_op jit(solution)/shard_map/rd,fd->rf/dot_general | solution.py:191
  399.8 8.2 multiply_convert_fusion.1
  410.0 13.6 %convolution_convert_fusion = bf16[2048,2048]{1,0:T(8,128)(2,1)} fusion(bf16[1024,2048]{1,0:T(8,128)(2,1)S(1)} %multiply_convert_fusion.1, bf16[1024,2048]{1,0:T(8,128)(2,1)} %all-gather.17.cloned.1.call-done), kind=kOutput, calls=%fused_computation.35 | convolution fusion | flops 8594128896 | bytes 16777216 | tf_op jit(solution)/shard_map/rf,rd->fd/dot_general | solution.py:187
  423.6 15.9 %convolution_convert_fusion.1 = bf16[2048,2048]{1,0:T(8,128)(2,1)} fusion(bf16[1024,2048]{1,0:T(8,128)(2,1)} %get-tuple-element.97, bf16[1024,2048]{1,0:T(8,128)(2,1)} %all-gather.7.cloned.1.call-done, f32[2048]{0:T(1024)S(1)} %bitcast.99, f32[2048]{0:T(1024)S(1)} %bitcast.92, f32[1024]{0:T(1024)S(1)} %add_rsqrt_fusion, f32[1024]{0:T(1024)S(1)} %broadcast_multiply_fusion.6), kind=kOutput, calls=%fused_computation.36 | convolution fusion | flops 8606711808 | bytes 16801792 | tf_op jit(solution)/shard_map/rd,rf->df/dot_general | solution.py:193
  441.4 11.2 fusion.77
  452.7 13.4 fusion.78
  466.1 12.8 fusion.76
  479.0 5.9 convolution_add_fusion.1
  490.0 60.8 %reduce-scatter.14.cloned.1.call-done = bf16[2048,256]{1,0:T(8,128)(2,1)} async-done(((bf16[2048,2048]{1,0:T(8,128)(2,1)}), bf16[2048,256]{1,0:T(8,128)(2,1)}) %reduce-scatter.14.cloned.1.call-update) | async-done | bytes 1048592 | tf_op jit(solution)/shard_map/reduce_scatter | solution.py:287
  553.5 72.3 %reduce-scatter.12.cloned.1.call-done = bf16[256,2048]{1,0:T(8,128)(2,1)} async-done(((bf16[2048,2048]{1,0:T(8,128)(2,1)}), bf16[256,2048]{1,0:T(8,128)(2,1)}) %reduce-scatter.12.cloned.1.call-update) | async-done | bytes 1048592 | tf_op jit(solution)/shard_map/reduce_scatter | solution.py:279
  628.6 563.1 %all-reduce.12.cloned.1.call-done = (f32[1024,2048]{1,0:T(8,128)}, f32[1024,2048]{1,0:T(8,128)}) async-done(((f32[1024,2048]{1,0:T(8,128)}, f32[1024,2048]{1,0:T(8,128)}), (f32[1024,2048]{1,0:T(8,128)}, f32[1024,2048]{1,0:T(8,128)})) %all-reduce.12.cloned.1.call-update) | async-done | bytes 16777232 | tf_op jit(solution)/shard_map/psum | solution.py:252
  1191.8 11.7 fusion.66
  1205.8 26.3 %all-reduce.8 = (f32[4,512]{1,0:T(4,128)S(1)}, f32[1536]{0:T(1024)}, f32[512]{0:T(512)S(1)}, f32[2048]{0:T(1024)}) all-reduce(f32[4,512]{1,0:T(4,128)S(1)} %pad_maximum_fusion.15, f32[1536]{0:T(1024)S(1)} %reduce_sum.200, f32[512]{0:T(512)S(1)} %get-tuple-element.121, ...), channel_id=1, replica_groups=mesh['fsdp'=4,'ctx'=2,'tp'=4] {'fsdp','ctx'}, use_global_device_ids=true, to_apply=%region_23.24 | all-reduce | flops 6144 | bytes 49152 | tf_op jit(solution)/shard_map/psum | solution.py:272
  1232.7 104.7 %reduce-scatter.6.cloned.1.call-done = f32[1024,512]{1,0:T(8,128)} async-done(((f32[1024,2048]{1,0:T(8,128)}), f32[1024,512]{1,0:T(8,128)}) %reduce-scatter.6.cloned.1.call-update) | async-done | bytes 2097168 | tf_op jit(solution)/shard_map/reduce_scatter | solution.py:177
  (228 shorter events, 139.6 us)
Async XLA Ops:
  7.2 30.3 %copy-start.46 = (s32[1,13]{1,0:T(1,128)S(1)}, s32[1,13]{1,0:T(1,128)}, u32[]{:S(2)}) copy-start(s32[1,13]{1,0:T(1,128)} %param.33) | copy-start | bytes 160
  7.2 86.1 %all-gather.7.cloned.1.call-start = ((), (), s32[]{:S(2)}) async-start(), calls=%async_computation.5 | async-start | bytes 5242880 | tf_op jit(solution)/shard_map/all_gather | solution.py:91
  7.9 131.4 %all-gather.9.cloned.1.call-start = ((), (), s32[]{:S(2)}) async-start(), calls=%async_computation.6 | async-start | bytes 7077888 | tf_op jit(solution)/shard_map/all_gather | solution.py:96
  8.7 168.8 %all-gather.11.cloned.1.call-start = ((), (), s32[]{:S(2)}) async-start(), calls=%async_computation.7 | async-start | bytes 2359296 | tf_op jit(solution)/shard_map/all_gather | solution.py:100
  9.4 242.2 %all-gather.17.cloned.1.call-start = ((), (), s32[]{:S(2)}) async-start(), calls=%async_computation.11 | async-start | bytes 5242880 | tf_op jit(solution)/shard_map/all_gather | solution.py:184
  10.0 335.5 %all-gather.13.cloned.1.call-start = ((), (), s32[]{:S(2)}) async-start(), calls=%async_computation.8 | async-start | bytes 9437184 | tf_op jit(solution)/shard_map/all_gather | solution.py:97
  10.6 355.4 %all-gather.15.cloned.1.call-start = ((), (), s32[]{:S(2)}) async-start(), calls=%async_computation.9 | async-start | bytes 9437184 | tf_op jit(solution)/shard_map/all_gather | solution.py:101
  11.1 474.5 %reduce-scatter.10.cloned.1.call-start = ((), (), s32[]{:S(2)}) async-start(), calls=%async_computation.13 | async-start | bytes 2359296 | tf_op jit(solution)/shard_map/reduce_scatter | solution.py:284
  35.0 296.7 %copy-start.37 = (f32[1,2048]{1,0:T(1,128)}, f32[1,2048]{1,0:T(1,128)S(1)}, u32[]{:S(2)}) copy-start(f32[1,2048]{1,0:T(1,128)S(1)} %get-tuple-element.129) | copy-start | bytes 24580
  37.5 131.5 %copy-start.12 = (f32[1024,32]{1,0:T(8,128)}, f32[1024,32]{1,0:T(8,128)S(1)}, u32[]{:S(2)}) copy-start(f32[1024,32]{1,0:T(8,128)S(1)} %get-tuple-element.137) | copy-start | bytes 393220
  37.5 131.5 %copy-start.14 = (f32[1024,32]{1,0:T(8,128)}, f32[1024,32]{1,0:T(8,128)S(1)}, u32[]{:S(2)}) copy-start(f32[1024,32]{1,0:T(8,128)S(1)} %get-tuple-element.138) | copy-start | bytes 393220
  174.2 88.4 %collective-permute-start.1 = (bf16[1024,2,256]{2,0,1:T(8,128)(2,1)}, bf16[1024,2,256]{2,0,1:T(8,128)(2,1)}, u32[]{:S(2)}, u32[]{:S(2)}) collective-permute-start(bf16[1024,2,256]{2,0,1:T(8,128)(2,1)} %pad_maximum_fusion.11), channel_id=1, source_target_pairs={{0,4},{1,5},{2,6},{3,7},{8,12},{9,13},{10,14},{11,15},{16,20},{17,... | collective-permute-start | bytes 3145736 | tf_op jit(solution)/shard_map/ppermute | solution.py:19
  259.8 20.7 %collective-permute-start = (bf16[1024,2,256]{0,2,1:T(8,128)(2,1)S(1)}, bf16[1024,2,256]{0,2,1:T(8,128)(2,1)S(1)}, u32[]{:S(2)}, u32[]{:S(2)}) collective-permute-start(bf16[1024,2,256]{0,2,1:T(8,128)(2,1)S(1)} %fusion.42), channel_id=1, source_target_pairs={{0,4},{1,5},{2,6},{3,7},{8,12},{9,13},{10,14},{11,15},{16,20},{17,... | collective-permute-start | bytes 3145736 | tf_op jit(solution)/shard_map/ppermute | solution.py:19
  262.6 21.3 %copy-start.22 = (bf16[1024,2,256]{2,0,1:T(8,128)(2,1)}, bf16[1024,2,256]{2,0,1:T(8,128)(2,1)S(1)}, u32[]{:S(2)}) copy-start(bf16[1024,2,256]{2,0,1:T(8,128)(2,1)S(1)} %pad_maximum_fusion.10) | copy-start | bytes 3145732
  278.8 46.6 %collective-permute-start.3 = (f32[1024,2,256]{2,0,1:T(8,128)}, f32[1024,2,256]{2,0,1:T(8,128)}, u32[]{:S(2)}, u32[]{:S(2)}) collective-permute-start(f32[1024,2,256]{2,0,1:T(8,128)} %slice.263), channel_id=1, source_target_pairs={{4,0},{5,1},{6,2},{7,3},{12,8},{13,9},{14,10},{15,11},{20,16},{21,... | collective-permute-start | bytes 6291464 | tf_op jit(solution)/shard_map/ppermute | solution.py:19
  301.7 17.4 %collective-permute-start.2 = (f32[1024,2,256]{2,0,1:T(8,128)}, f32[1024,2,256]{2,0,1:T(8,128)}, u32[]{:S(2)}, u32[]{:S(2)}) collective-permute-start(f32[1024,2,256]{2,0,1:T(8,128)} %slice.261), channel_id=1, source_target_pairs={{4,0},{5,1},{6,2},{7,3},{12,8},{13,9},{14,10},{15,11},{20,16},{21,... | collective-permute-start | bytes 6291464 | tf_op jit(solution)/shard_map/ppermute | solution.py:19
  312.0 175.4 %reduce-scatter.8.cloned.1.call-start = ((), (), s32[]{:S(2)}) async-start(), calls=%async_computation.12 | async-start | bytes 7077888 | tf_op jit(solution)/shard_map/reduce_scatter | solution.py:276
  345.4 205.4 %reduce-scatter.14.cloned.1.call-start = ((), (), s32[]{:S(2)}) async-start(), calls=%async_computation.15 | async-start | bytes 9437184 | tf_op jit(solution)/shard_map/reduce_scatter | solution.py:287
  423.6 202.2 %reduce-scatter.12.cloned.1.call-start = ((), (), s32[]{:S(2)}) async-start(), calls=%async_computation.14 | async-start | bytes 9437184 | tf_op jit(solution)/shard_map/reduce_scatter | solution.py:279
  439.6 752.2 %all-reduce.12.cloned.1.call-start = ((), (), s32[]{:S(2)}) async-start(), calls=%async_computation.16 | async-start | bytes 33554432 | tf_op jit(solution)/shard_map/psum | solution.py:252
  466.1 871.4 %reduce-scatter.6.cloned.1.call-start = ((), (), s32[]{:S(2)}) async-start(), calls=%async_computation.10 | async-start | bytes 10485760 | tf_op jit(solution)/shard_map/reduce_scatter | solution.py:177
  484.9 706.9 %copy-start.38 = (f32[1,2048]{1,0:T(1,128)S(1)}, f32[1,2048]{1,0:T(1,128)}, u32[]{:S(2)}) copy-start(f32[1,2048]{1,0:T(1,128)} %copy-done.37) | copy-start | bytes 24580
  1203.5 134.0 %copy-start.18 = (bf16[1024,512]{1,0:T(8,128)(2,1)S(1)}, bf16[1024,512]{1,0:T(8,128)(2,1)}, u32[]{:S(2)}) copy-start(bf16[1024,512]{1,0:T(8,128)(2,1)} %param.29) | copy-start | bytes 3145732
  1232.1 108.9 %copy-start.42 = (f32[512]{0:T(512)}, f32[512]{0:T(512)S(1)}, u32[]{:S(2)}) copy-start(f32[512]{0:T(512)S(1)} %get-tuple-element.178) | copy-start | bytes 6148
  (42 other events, 192.2 us)
Sparse Core Ops, SparseCore 0:
  9.6 83.6 all-gather.6
  95.1 44.1 all-gather.8
  141.2 28.1 all-gather.10
  170.8 80.7 all-gather.16
  253.4 52.9 all-gather.12
  308.1 57.9 all-gather.14
  369.3 41.2 reduce-scatter.9
  414.3 61.7 reduce-scatter.7
  479.5 71.2 reduce-scatter.13
  554.5 71.2 reduce-scatter.11
  628.5 563.2 all-reduce.11
  1194.0 143.4 reduce-scatter.5
where the time goes:
time: 1350 us
  waiting for transfers between devices  976 us (72%)
  matrix products  195 us (14%)
  other arithmetic  68.2 us (5%)
  local copies, waits for them, and re-layouts  42.9 us (3%)
  blocking collectives  41.4 us (3%)
  between operations  15.3 us (1%)
    psum x1, waiting for transfers between devices, on_device(): total_attn, total_ffn = lax.psum((grad_attn_in, grad_ffn_in), 'tp')  563 us
    reduce_scatter x1, waiting for transfers between devices, on_device(): lax.psum_scatter(partial_out, 'tp', scatter_dimension=1, tiled=True)  105 us
    all_gather x1, waiting for transfers between devices, on_device(): cotangent = lax.all_gather(out_grad, 'tp', axis=1, tiled=True)  74.1 us
    reduce_scatter x1, waiting for transfers between devices, on_device(): lax.psum_scatter(grad_up_w.astype(jnp.bfloat16), ('fsdp', 'ctx'), scatter...  72.3 us
    reduce_scatter x1, waiting for transfers between devices, on_device(): lax.psum_scatter(grad_down_w.astype(jnp.bfloat16), ('fsdp', 'ctx'), scatt...  60.8 us
    all_gather x1, waiting for transfers between devices, on_device(): lax.all_gather(residual, 'tp', axis=1, tiled=True)  50.9 us
    all_gather x1, waiting for transfers between devices, on_device(): lax.all_gather(qkv_weight, ('fsdp', 'ctx'), axis=0, tiled=True)  41.3 us
    dot_general x1, matrix products, on_device(): jnp.einsum('rd,fd->rf', cotangent, down_full, preferred_element_type=jnp....  33.7 us
  transfers between devices with their start and end apart: 16, of which 8 were waited for; matrix products, arithmetic and copies ran while one was open for 22% of the time, Pallas kernels for 0%

commit v1 on v0

--- a/solution.py
+++ b/solution.py
@@ -181,7 +181,12 @@
         + dense_bias.astype(jnp.float32)
         + down_bias.astype(jnp.float32)
     ).astype(jnp.bfloat16)
-    cotangent = lax.all_gather(out_grad, "tp", axis=1, tiled=True)
+    ring = [out_grad]
+    for hop in range(3):
+        ring.append(lax.ppermute(ring[-1], "tp", [(dev, (dev + 1) % 4) for dev in range(4)]))
+    cotangent = jnp.roll(
+        jnp.concatenate(ring[::-1], axis=1), (lax.axis_index("tp") + 1) * ring[0].shape[1], axis=1
+    )
     grad_out_bias = jnp.sum(out_grad.astype(jnp.float32), axis=0)
     grad_dense_w = jnp.einsum("rf,rd->fd", attended, cotangent, preferred_element_type=jnp.float32)
     grad_down_w = jnp.einsum("rf,rd->fd", hidden, cotangent, preferred_element_type=jnp.float32)

time: 1350 us -> 1310 us (0.970)
  waiting for transfers between devices: 976 us -> 848 us
  blocking collectives: 41.4 us -> 91.9 us
  starting transfers between devices: 8.72 us -> 26.3 us
    all_gather x1 -> x0, waiting for transfers between devices: 74.1 us -> none  [on_device(): cotangent = lax.all_gather(out_grad, 'tp', axis=1, tiled=True)]
    ppermute x0 -> x3, waiting for transfers between devices: none -> 51.8 us  [on_device(): lax.ppermute(ring[-1], 'tp', [(dev, (dev + 1) % 4) for dev in range(4)])]
    all_gather x1, waiting for transfers between devices: 50.9 us -> 0.01 us  [on_device(): lax.all_gather(residual, 'tp', axis=1, tiled=True)]
    all_gather x1, blocking collectives: 15.1 us -> 65.7 us  [on_device(): lax.all_gather(norm_stack, 'tp', axis=1, tiled=True)]
    all_gather x1, waiting for transfers between devices: 41.3 us -> 0.02 us  [on_device(): lax.all_gather(qkv_weight, ('fsdp', 'ctx'), axis=0, tiled=True)]
    dot_general x1, matrix products: 14.9 us -> 34.1 us  [on_device(): jnp.dot(ffn_in, up_full, preferred_element_type=jnp.float32)]
    ppermute x0 -> x3, starting transfers between devices: none -> 18.9 us  [on_device(): lax.ppermute(ring[-1], 'tp', [(dev, (dev + 1) % 4) for dev in range(4)])]
    unnamed x103 -> x112, local copies, waits for them, and re-layouts: 15.9 us -> 28.7 us
  transfers between devices with their start and end apart: 16 -> 18, of which waited for: 8 -> 6; matrix products, arithmetic and copies ran while one was open for 22% -> 23% of each run, Pallas kernels for 0% -> 0%
where the time goes in v1:
time: 1310 us; the launch traced here: 1300 us
  waiting for transfers between devices  848 us (65%)
  matrix products  204 us (16%)
  blocking collectives  91.9 us (7%)
  other arithmetic  58.8 us (4%)
  local copies, waits for them, and re-layouts  56.3 us (4%)
  starting transfers between devices  26.3 us (2%)
  between operations  15.2 us (1%)
    psum x1, waiting for transfers between devices, on_device(): total_attn, total_ffn = lax.psum((grad_attn_in, grad_ffn_in), 'tp')  563 us
    reduce_scatter x1, waiting for transfers between devices, on_device(): lax.psum_scatter(partial_out, 'tp', scatter_dimension=1, tiled=True)  105 us
    reduce_scatter x1, waiting for transfers between devices, on_device(): lax.psum_scatter(grad_up_w.astype(jnp.bfloat16), ('fsdp', 'ctx'), scatter...  72.4 us
    all_gather x1, blocking collectives, on_device(): lax.all_gather(norm_stack, 'tp', axis=1, tiled=True)  65.7 us
    reduce_scatter x1, waiting for transfers between devices, on_device(): lax.psum_scatter(grad_down_w.astype(jnp.bfloat16), ('fsdp', 'ctx'), scatt...  53.2 us
    ppermute x3, waiting for transfers between devices, on_device(): lax.ppermute(ring[-1], 'tp', [(dev, (dev + 1) % 4) for dev in range(4)])  51.8 us
    dot_general x1, matrix products, on_device(): jnp.dot(ffn_in, up_full, preferred_element_type=jnp.float32)  34.1 us
    unnamed x112, local copies, waits for them, and re-layouts  28.7 us
  transfers between devices with their start and end apart: 18, of which 6 were waited for; matrix products, arithmetic and copies ran while one was open for 23% of the time, Pallas kernels for 0%

profile of v1, /device:TPU:0, one launch (start us, length us, event | category | flops | bytes accessed | tf_op | source)
XLA Modules:
  0.0 1300.8 jit_solution(5261138258798441410)
XLA Ops:
  18.6 34.0 %collective-permute-done.2 = bf16[1024,512]{1,0:T(8,128)(2,1)S(1)} collective-permute-done((bf16[1024,512]{1,0:T(8,128)(2,1)}, bf16[1024,512]{1,0:T(8,128)(2,1)S(1)}, u32[]{:S(2)}, u32[]{:S(2)}) %collective-permute-start.2) | collective-permute-done | bytes 1048608 | tf_op jit(solution)/shard_map/ppermute | solution.py:186
  52.6 14.3 %collective-permute-start.3 = (bf16[1024,512]{1,0:T(8,128)(2,1)S(1)}, bf16[1024,512]{1,0:T(8,128)(2,1)}, u32[]{:S(2)}, u32[]{:S(2)}) collective-permute-start(bf16[1024,512]{1,0:T(8,128)(2,1)S(1)} %collective-permute-done.2), channel_id=1, source_target_pairs={{0,1},{1,2},{2,3},{3,0},{4,5},{5,6},{6,7},{7,4},{8,9},{9,10},{10,1... | collective-permute-start | bytes 3145736 | tf_op jit(solution)/shard_map/ppermute | solution.py:186
  68.3 65.7 %all_gather.19 = bf16[4,2048]{1,0:T(4,128)(2,1)S(1)} all-gather(bf16[4,512]{1,0:T(4,128)(2,1)S(1)} %pad_maximum_fusion.16), channel_id=1, replica_groups=mesh['fsdp'=4,'ctx'=2,'tp'=4] {'tp'}, dimensions={1}, use_global_device_ids=true | all-gather | bytes 20480 | tf_op jit(solution)/shard_map/all_gather | solution.py:92
  144.2 17.7 %collective-permute-done.4 = bf16[1024,512]{1,0:T(8,128)(2,1)} collective-permute-done((bf16[1024,512]{1,0:T(8,128)(2,1)}, bf16[1024,512]{1,0:T(8,128)(2,1)}, u32[]{:S(2)}, u32[]{:S(2)}) %collective-permute-start.4) | collective-permute-done | bytes 1048608 | tf_op jit(solution)/shard_map/ppermute | solution.py:186
  180.4 12.6 convolution_add_fusion
  193.0 6.6 copy.87
  217.6 5.2 fusion.39
  258.3 5.3 bitcast_add_fusion.1
  273.7 6.0 convolution_convert_fusion.3
  299.5 13.6 %convolution_convert_fusion.2 = bf16[2048,1536]{1,0:T(8,128)(2,1)} fusion(bf16[1024,1536]{0,1:T(8,128)(2,1)} %bitcast.82, bf16[1024,2048]{1,0:T(8,128)(2,1)} %all-gather.6.cloned.1.call-done, f32[2048]{0:T(1024)S(1)} %bitcast.97, f32[2048]{0:T(1024)S(1)} %bitcast.85, f32[1024]{0:T(1024)S(1)} %add_rsqrt_fusion, f32[1024]{0:T(1024)S(1)} %broadcast_multiply_fusion.6), kind=kOutput, calls=%fused_computation.37 | convolution fusion | flops 6458179584 | bytes 13656064 | tf_op jit(solution)/shard_map/rd,rf->df/dot_general | solution.py:252
  313.9 34.1 %multiply_convert_fusion.1 = (bf16[1024,2048]{1,0:T(8,128)(2,1)S(1)}, f32[1024,2048]{1,0:T(8,128)}, f32[1024,2048]{1,0:T(8,128)}) fusion(f32[2048]{0:T(1024)S(1)} %convert_element_type.150, bf16[2048,2048]{1,0:T(8,128)(2,1)} %all-gather.12.cloned.1.call-done, bf16[1024,2048]{1,0:T(8,128)(2,1)} %all-gather.6.cloned.1.call-done, f32[2048]{0:T(1024)S(1)} %bitcast.94, ...), kind=kOutput, calls=%fused_computation.16 | convolution fusion | flops 8740929536 | bytes 33587200 | tf_op jit(solution)/shard_map/dot_general | solution.py:169
  350.0 13.7 %convolution_convert_fusion = bf16[2048,2048]{1,0:T(8,128)(2,1)} fusion(bf16[1024,2048]{1,0:T(8,128)(2,1)S(1)} %get-tuple-element.100, bf16[1024,4096]{1,0:T(8,128)(2,1)} %constant_dynamic-update-slice_fusion, s32[]{:T(128)S(6)} %select_n.39), kind=kOutput, calls=%fused_computation.35 | convolution fusion | flops 8594128896 | bytes 16777220 | tf_op jit(solution)/shard_map/rf,rd->fd/dot_general | solution.py:192
  363.8 20.3 %convert_reduce_fusion.1 = (f32[2048]{0:T(1024)S(1)}, bf16[1024,2048]{1,0:T(8,128)(2,1)}) fusion(f32[1024,2048]{1,0:T(8,128)} %get-tuple-element.101, bf16[2048,2048]{1,0:T(8,128)(2,1)} %all-gather.14.cloned.1.call-done, bf16[1024,4096]{1,0:T(8,128)(2,1)} %constant_dynamic-update-slice_fusion, s32[]{:T(128)S(6)} %select_n.39, ...), kind=kOutput, calls=%fused_computation.7 | convolution fusion | flops 8625584128 | bytes 33570820 | tf_op jit(solution)/shard_map/rd,fd->rf/dot_general | solution.py:196
  384.2 14.1 %convolution_convert_fusion.1 = bf16[2048,2048]{1,0:T(8,128)(2,1)} fusion(bf16[1024,2048]{1,0:T(8,128)(2,1)} %get-tuple-element.150, bf16[1024,2048]{1,0:T(8,128)(2,1)S(1)} %copy-done.1, f32[2048]{0:T(1024)S(1)} %bitcast.95, f32[2048]{0:T(1024)S(1)} %bitcast.88, f32[1024]{0:T(1024)S(1)} %add_rsqrt_fusion, f32[1024]{0:T(1024)S(1)} %broadcast_multiply_fusion.6), kind=kOutput, calls=%fused_computation.36 | convolution fusion | flops 8606711808 | bytes 16801792 | tf_op jit(solution)/shard_map/rd,rf->df/dot_general | solution.py:198
  400.3 11.3 fusion.92
  411.6 13.4 %fusion.93 = f32[1024,2048]{1,0:T(8,128)} fusion(bf16[1024,2048]{1,0:T(8,128)(2,1)S(1)} %copy-done.50, bf16[2048,2048]{1,0:T(8,128)(2,1)} %all-gather.12.cloned.1.call-done), kind=kOutput, calls=%fused_computation.196 | convolution fusion | flops 8589934592 | bytes 20971520 | tf_op jit(solution)/shard_map/rf,df->rd/dot_general | solution.py:200
  425.0 13.0 fusion.91
  438.0 7.1 convolution_add_fusion.1
  450.3 53.2 %reduce-scatter.14.cloned.1.call-done = bf16[2048,256]{1,0:T(8,128)(2,1)} async-done(((bf16[2048,2048]{1,0:T(8,128)(2,1)}), bf16[2048,256]{1,0:T(8,128)(2,1)}) %reduce-scatter.14.cloned.1.call-update) | async-done | bytes 1048592 | tf_op jit(solution)/shard_map/reduce_scatter | solution.py:292
  506.2 72.4 %reduce-scatter.12.cloned.1.call-done = bf16[256,2048]{1,0:T(8,128)(2,1)} async-done(((bf16[2048,2048]{1,0:T(8,128)(2,1)}), bf16[256,2048]{1,0:T(8,128)(2,1)}) %reduce-scatter.12.cloned.1.call-update) | async-done | bytes 1048592 | tf_op jit(solution)/shard_map/reduce_scatter | solution.py:284
  581.4 563.0 %all-reduce.12.cloned.1.call-done = (f32[1024,2048]{1,0:T(8,128)}, f32[1024,2048]{1,0:T(8,128)}) async-done(((f32[1024,2048]{1,0:T(8,128)}, f32[1024,2048]{1,0:T(8,128)}), (f32[1024,2048]{1,0:T(8,128)}, f32[1024,2048]{1,0:T(8,128)})) %all-reduce.12.cloned.1.call-update) | async-done | bytes 16777232 | tf_op jit(solution)/shard_map/psum | solution.py:257
  1144.5 11.8 fusion.81
  1158.6 26.2 %all-reduce.8 = (f32[4,512]{1,0:T(4,128)S(1)}, f32[1536]{0:T(1024)}, f32[512]{0:T(512)S(1)}, f32[2048]{0:T(1024)}) all-reduce(f32[4,512]{1,0:T(4,128)S(1)} %pad_maximum_fusion.15, f32[1536]{0:T(1024)S(1)} %reduce_sum.200, f32[512]{0:T(512)S(1)} %get-tuple-element.120, ...), channel_id=1, replica_groups=mesh['fsdp'=4,'ctx'=2,'tp'=4] {'fsdp','ctx'}, use_global_device_ids=true, to_apply=%region_23.24 | all-reduce | flops 6144 | bytes 49152 | tf_op jit(solution)/shard_map/psum | solution.py:277
  1185.4 104.9 %reduce-scatter.6.cloned.1.call-done = f32[1024,512]{1,0:T(8,128)} async-done(((f32[1024,2048]{1,0:T(8,128)}), f32[1024,512]{1,0:T(8,128)}) %reduce-scatter.6.cloned.1.call-update) | async-done | bytes 2097168 | tf_op jit(solution)/shard_map/reduce_scatter | solution.py:177
  (240 shorter events, 145.9 us)
Async XLA Ops:
  7.2 168.5 %all-gather.6.cloned.1.call-start = ((), (), s32[]{:S(2)}) async-start(), calls=%async_computation.5 | async-start | bytes 5242880 | tf_op jit(solution)/shard_map/all_gather | solution.py:91
  7.9 132.9 %copy-start.46 = (s32[1,13]{1,0:T(1,128)S(1)}, s32[1,13]{1,0:T(1,128)}, u32[]{:S(2)}) copy-start(s32[1,13]{1,0:T(1,128)} %param.33) | copy-start | bytes 160
  7.9 172.4 %all-gather.8.cloned.1.call-start = ((), (), s32[]{:S(2)}) async-start(), calls=%async_computation.6 | async-start | bytes 7077888 | tf_op jit(solution)/shard_map/all_gather | solution.py:96
  8.7 208.9 %all-gather.10.cloned.1.call-start = ((), (), s32[]{:S(2)}) async-start(), calls=%async_computation.7 | async-start | bytes 2359296 | tf_op jit(solution)/shard_map/all_gather | solution.py:100
  9.4 304.4 %all-gather.12.cloned.1.call-start = ((), (), s32[]{:S(2)}) async-start(), calls=%async_computation.8 | async-start | bytes 9437184 | tf_op jit(solution)/shard_map/all_gather | solution.py:97
  10.0 353.8 %all-gather.14.cloned.1.call-start = ((), (), s32[]{:S(2)}) async-start(), calls=%async_computation.9 | async-start | bytes 9437184 | tf_op jit(solution)/shard_map/all_gather | solution.py:101
  10.0 42.6 %collective-permute-start.2 = (bf16[1024,512]{1,0:T(8,128)(2,1)}, bf16[1024,512]{1,0:T(8,128)(2,1)S(1)}, u32[]{:S(2)}, u32[]{:S(2)}) collective-permute-start(bf16[1024,512]{1,0:T(8,128)(2,1)} %param.30), channel_id=1, source_target_pairs={{0,1},{1,2},{2,3},{3,0},{4,5},{5,6},{6,7},{7,4},{8,9},{9,10},{10,1... | collective-permute-start | bytes 3145736 | tf_op jit(solution)/shard_map/ppermute | solution.py:186
  13.1 432.8 %reduce-scatter.10.cloned.1.call-start = ((), (), s32[]{:S(2)}) async-start(), calls=%async_computation.12 | async-start | bytes 2359296 | tf_op jit(solution)/shard_map/reduce_scatter | solution.py:289
  52.6 84.7 %collective-permute-start.3 = (bf16[1024,512]{1,0:T(8,128)(2,1)S(1)}, bf16[1024,512]{1,0:T(8,128)(2,1)}, u32[]{:S(2)}, u32[]{:S(2)}) collective-permute-start(bf16[1024,512]{1,0:T(8,128)(2,1)S(1)} %collective-permute-done.2), channel_id=1, source_target_pairs={{0,1},{1,2},{2,3},{3,0},{4,5},{5,6},{6,7},{7,4},{8,9},{9,10},{10,1... | collective-permute-start | bytes 3145736 | tf_op jit(solution)/shard_map/ppermute | solution.py:186
  137.4 24.5 %collective-permute-start.4 = (bf16[1024,512]{1,0:T(8,128)(2,1)}, bf16[1024,512]{1,0:T(8,128)(2,1)}, u32[]{:S(2)}, u32[]{:S(2)}) collective-permute-start(bf16[1024,512]{1,0:T(8,128)(2,1)} %collective-permute-done.3), channel_id=1, source_target_pairs={{0,1},{1,2},{2,3},{3,0},{4,5},{5,6},{6,7},{7,4},{8,9},{9,10},{10,1... | collective-permute-start | bytes 3145736 | tf_op jit(solution)/shard_map/ppermute | solution.py:186
  140.8 69.2 %copy-start.15 = (f32[1024,32]{1,0:T(8,128)}, f32[1024,32]{1,0:T(8,128)S(1)}, u32[]{:S(2)}) copy-start(f32[1024,32]{1,0:T(8,128)S(1)} %get-tuple-element.136) | copy-start | bytes 393220
  144.2 155.4 %copy-start.37 = (f32[1,2048]{1,0:T(1,128)}, f32[1,2048]{1,0:T(1,128)S(1)}, u32[]{:S(2)}) copy-start(f32[1,2048]{1,0:T(1,128)S(1)} %get-tuple-element.128) | copy-start | bytes 24580
  215.3 12.8 collective-permute-start.1
  225.4 20.3 %collective-permute-start = (bf16[1024,2,256]{0,2,1:T(8,128)(2,1)S(1)}, bf16[1024,2,256]{0,2,1:T(8,128)(2,1)S(1)}, u32[]{:S(2)}, u32[]{:S(2)}) collective-permute-start(bf16[1024,2,256]{0,2,1:T(8,128)(2,1)S(1)} %fusion.53), channel_id=1, source_target_pairs={{0,4},{1,5},{2,6},{3,7},{8,12},{9,13},{10,14},{11,15},{16,20},{17,... | collective-permute-start | bytes 3145736 | tf_op jit(solution)/shard_map/ppermute | solution.py:19
  244.2 48.7 %collective-permute-start.6 = (f32[1024,2,256]{2,0,1:T(8,128)}, f32[1024,2,256]{2,0,1:T(8,128)}, u32[]{:S(2)}, u32[]{:S(2)}) collective-permute-start(f32[1024,2,256]{2,0,1:T(8,128)} %slice.263), channel_id=1, source_target_pairs={{4,0},{5,1},{6,2},{7,3},{12,8},{13,9},{14,10},{15,11},{20,16},{21,... | collective-permute-start | bytes 6291464 | tf_op jit(solution)/shard_map/ppermute | solution.py:19
  267.1 19.6 %collective-permute-start.5 = (f32[1024,2,256]{2,0,1:T(8,128)}, f32[1024,2,256]{2,0,1:T(8,128)}, u32[]{:S(2)}, u32[]{:S(2)}) collective-permute-start(f32[1024,2,256]{2,0,1:T(8,128)} %slice.261), channel_id=1, source_target_pairs={{4,0},{5,1},{6,2},{7,3},{12,8},{13,9},{14,10},{15,11},{20,16},{21,... | collective-permute-start | bytes 6291464 | tf_op jit(solution)/shard_map/ppermute | solution.py:19
  279.8 168.0 %reduce-scatter.8.cloned.1.call-start = ((), (), s32[]{:S(2)}) async-start(), calls=%async_computation.11 | async-start | bytes 7077888 | tf_op jit(solution)/shard_map/reduce_scatter | solution.py:281
  313.2 190.3 %reduce-scatter.14.cloned.1.call-start = ((), (), s32[]{:S(2)}) async-start(), calls=%async_computation.14 | async-start | bytes 9437184 | tf_op jit(solution)/shard_map/reduce_scatter | solution.py:292
  363.7 214.9 %reduce-scatter.12.cloned.1.call-start = ((), (), s32[]{:S(2)}) async-start(), calls=%async_computation.13 | async-start | bytes 9437184 | tf_op jit(solution)/shard_map/reduce_scatter | solution.py:284
  398.3 746.2 %all-reduce.12.cloned.1.call-start = ((), (), s32[]{:S(2)}) async-start(), calls=%async_computation.15 | async-start | bytes 33554432 | tf_op jit(solution)/shard_map/psum | solution.py:257
  425.0 865.3 %reduce-scatter.6.cloned.1.call-start = ((), (), s32[]{:S(2)}) async-start(), calls=%async_computation.10 | async-start | bytes 10485760 | tf_op jit(solution)/shard_map/reduce_scatter | solution.py:177
  445.2 699.2 %copy-start.38 = (f32[1,2048]{1,0:T(1,128)S(1)}, f32[1,2048]{1,0:T(1,128)}, u32[]{:S(2)}) copy-start(f32[1,2048]{1,0:T(1,128)} %copy-done.37) | copy-start | bytes 24580
  1156.2 134.1 %copy-start.19 = (bf16[1024,512]{1,0:T(8,128)(2,1)S(1)}, bf16[1024,512]{1,0:T(8,128)(2,1)}, u32[]{:S(2)}) copy-start(bf16[1024,512]{1,0:T(8,128)(2,1)} %param.29) | copy-start | bytes 3145732
  1184.8 109.0 %copy-start.43 = (f32[512]{0:T(512)}, f32[512]{0:T(512)S(1)}, u32[]{:S(2)}) copy-start(f32[512]{0:T(512)S(1)} %get-tuple-element.180) | copy-start | bytes 6148
  (45 other events, 307.5 us)
Sparse Core Ops, SparseCore 0:
  9.6 119.3 all-gather.5
  130.9 43.8 all-gather.7
  176.7 28.1 all-gather.9
  206.6 54.3 all-gather.11
  262.8 55.9 all-gather.13
  321.9 41.2 reduce-scatter.9
  366.9 61.7 reduce-scatter.7
  432.2 71.2 reduce-scatter.13
  507.4 71.2 reduce-scatter.11
  581.1 563.2 all-reduce.11
  1146.8 143.4 reduce-scatter.5
